TPU v7x, 32 devices: a whole 2x2x4 slice. The times are simulated.
32 devices in a mesh: samp: 8 (over y, x, core), exp: 4 (over z).
Axes of the slice: x: 2, y: 2, z: 4, core: 2. Of those that a mesh axis runs over, the one named last changes fastest.
Arguments:
- prompt_states: bfloat16 [4, 8, 64, 2048], P('exp', 'samp'), may hold values from -6 to 6
- edit_offsets: bfloat16 [1, 4, 8, 64, 2048], P(None, 'exp', 'samp'), may hold values from -6 to 6
- targets: bfloat16 [2, 4, 8, 64, 2048], P(None, 'exp', 'samp'), may hold values from -6 to 6
- router: bfloat16 [2048, 32], replicated, may hold values from -0.125 to 0.125
- route_ids: int32 [2, 4, 8, 64, 8], P(None, 'exp', 'samp'), may hold values from 0 to 31, all different within a row; in each aligned block of 64 rows (0 to 63, 64 to 127, ..., all dimensions but the last counted through in order) at most 20 rows name the same one
- chosen: int32 [1, 4], replicated, may hold values from 0 to 7
- lengths: int32 [2, 4, 8], P(None, 'exp', 'samp'), may hold values from 16 to 64, as said below
- w_gate: bfloat16 [32, 2048, 768], P(('samp', 'exp')), may hold values from -0.125 to 0.125
- w_up: bfloat16 [32, 2048, 768], P(('samp', 'exp')), may hold values from -0.125 to 0.125
- w_down: bfloat16 [32, 768, 2048], P(('samp', 'exp')), may hold values from -0.21875 to 0.21875
Outputs:
- grad_gate: bfloat16 [32, 2048, 768], P(('samp', 'exp'))
- grad_up: bfloat16 [32, 2048, 768], P(('samp', 'exp'))
- grad_down: bfloat16 [32, 768, 2048], P(('samp', 'exp'))
- advantages: float32 [2, 4, 8], P(None, 'exp', 'samp')
Inputs may be any that keep to these rules, and one draw needn't show every extreme that they name: `route_ids`: in each block of 64 rows that one repair has in one round, the 8 ids of a row differ, no expert is named by more than 20 rows, a bound that some block reaches. `lengths`: in each round and prompt some sample has exactly 64 scored tokens.
All inputs are finite; a program needn't handle non-finite values.
Results may differ from a plain program's by a relative error of at most 0.015.
Values may be sent and summed in bfloat16 or wider, within the bound.
A program may use at most 128 MiB of HBM per device.

v0:
```python
import functools
import math

import jax
import jax.numpy as jnp
from jax import lax
from jax.experimental import pallas as pl
from jax.experimental.pallas import tpu as pltpu
from jax.sharding import PartitionSpec as P

F32 = jnp.float32
BF16 = jnp.bfloat16


def dot(a, b):
    return jnp.dot(a, b, preferred_element_type=F32)


def dot_tn(a, b):
    return lax.dot_general(a, b, (((0,), (0,)), ((), ())), preferred_element_type=F32)


def dot_nt(a, b):
    return lax.dot_general(a, b, (((1,), (1,)), ((), ())), preferred_element_type=F32)


MESH = pl.DeviceIdType.MESH
VMEM = pl.BlockSpec(memory_space=pltpu.VMEM)
ANY = pl.BlockSpec(memory_space=pl.ANY)


def greet(peers):
    barrier = pltpu.get_barrier_semaphore()
    for peer in peers:
        pl.semaphore_signal(barrier, inc=1, device_id=peer, device_id_type=MESH)
    pl.semaphore_wait(barrier, len(peers))


def remote(src, dst, send, recv, peer):
    return pltpu.make_async_remote_copy(
        src_ref=src, dst_ref=dst, send_sem=send, recv_sem=recv, device_id=peer, device_id_type=MESH
    )


def dispatch_kernel(ns, ng, seq, block, rounds, *refs):
    count = 2 * rounds
    code_ref, ins, outs = refs[0], refs[1 : 1 + count], refs[1 + count : 1 + 2 * count]
    rest = refs[1 + 2 * count :]
    codes, alls, sends = rest[0], rest[1 : 1 + count], rest[1 + count : 1 + 2 * count]
    place, gs, gr, ss, sr, own_sem = rest[1 + 2 * count :]
    me_s, me_g = lax.axis_index("samp"), lax.axis_index("exp")
    exp_peers = [(me_s, lax.rem(me_g + k, ng)) for k in range(1, ng)]
    samp_peers = [(lax.rem(me_s + k, ns), me_g) for k in range(1, ns)]
    greet(exp_peers + samp_peers)
    mine = pl.ds(pl.multiple_of(me_g * seq, seq), seq)
    code_copies = []
    for k, peer in enumerate(exp_peers):
        copy = remote(
            code_ref.at[peer[1]], codes.at[me_g], gs.at[count, k], gr.at[count, k], peer
        )
        copy.start()
        code_copies.append(copy)
    copies = []
    for i in range(count):
        here = []
        for k, peer in enumerate(exp_peers):
            copy = remote(ins[i], alls[i].at[mine, :], gs.at[i, k], gr.at[i, k], peer)
            copy.start()
            here.append(copy)
        copies.append(here)
    codes[me_g] = code_ref[me_g]
    for i in range(count):
        alls[i][mine, :] = ins[i][...]
    for copy in code_copies:
        copy.wait()
    slots = lax.broadcasted_iota(jnp.int32, (block, ng * seq), 0).astype(F32)
    for r in range(rounds):
        line = jnp.concatenate([codes[g][:, r * seq : (r + 1) * seq] for g in range(ng)], axis=1)
        for d in range(ns):
            hit = jnp.where(line[d : d + 1, :] == slots, 1.0, 0.0)
            place[r, d * block : (d + 1) * block, :] = hit.astype(BF16)
    home = pl.ds(pl.multiple_of(me_s * block, block), block)
    for i in range(count):
        for copy in copies[i]:
            copy.wait()

        def put(d, i=i):
            part = pl.ds(pl.multiple_of(d * block, block), block)
            sends[i][part, :] = dot(place[i // 2, part, :], alls[i][...]).astype(BF16)
            return part

        def step(k, carry, i=i, put=put):
            d = lax.rem(me_s + k, ns)
            part = put(d)
            remote(
                sends[i].at[part, :], outs[i].at[home, :], ss.at[i, k], sr.at[i, k], (d, me_g)
            ).start()
            return carry

        lax.fori_loop(1, ns, step, 0)
        put(me_s)
        pltpu.make_async_copy(sends[i].at[home, :], outs[i].at[home, :], own_sem.at[i]).start()
    for i in range(count):

        def finish(k, carry, i=i):
            d = lax.rem(me_s + k, ns)
            part = pl.ds(pl.multiple_of(d * block, block), block)
            remote(
                sends[i].at[part, :], outs[i].at[home, :], ss.at[i, k], sr.at[i, k], (d, me_g)
            ).wait()
            return carry

        lax.fori_loop(1, ns, finish, 0)
        pltpu.make_async_copy(sends[i].at[home, :], outs[i].at[home, :], own_sem.at[i]).wait()


def dispatch(code, arrays, ns, ng, seq, block, rounds):
    count = len(arrays)
    widths = [a.shape[1] for a in arrays]
    return pl.pallas_call(
        functools.partial(dispatch_kernel, ns, ng, seq, block, rounds),
        out_shape=[jax.ShapeDtypeStruct((ns * block, w), BF16) for w in widths],
        in_specs=[VMEM] * (1 + count),
        out_specs=[ANY] * count,
        scratch_shapes=[pltpu.VMEM(code.shape, F32)]
        + [pltpu.VMEM((ng * seq, w), BF16) for w in widths]
        + [pltpu.VMEM((ns * block, w), BF16) for w in widths]
        + [
            pltpu.VMEM((rounds, ns * block, ng * seq), BF16),
            pltpu.SemaphoreType.DMA((count + 1, ng - 1)),
            pltpu.SemaphoreType.DMA((count + 1, ng - 1)),
            pltpu.SemaphoreType.DMA((count, ns)),
            pltpu.SemaphoreType.DMA((count, ns)),
            pltpu.SemaphoreType.DMA((count,)),
        ],
        compiler_params=pltpu.CompilerParams(
            collective_id=0, has_side_effects=True, vmem_limit_bytes=48 * 2**20
        ),
    )(code, *arrays)


def mix_kernel(ns, ng, part_ref, out_ref, rows_in, half, cols_in, final, sems_a, sems_b):
    me_s, me_g = lax.axis_index("samp"), lax.axis_index("exp")
    exp_peers = [(me_s, lax.rem(me_g + k, ng)) for k in range(1, ng)]
    samp_peers = [(lax.rem(me_s + k, ns), me_g) for k in range(1, ns)]
    greet(exp_peers + samp_peers)
    high, width = rows_in.shape[1], rows_in.shape[2]
    wide = width // ng

    def rows_of(d):
        return pl.ds(pl.multiple_of(d * high, high), high)

    def cols_of(g):
        return pl.ds(pl.multiple_of(g * wide, wide), wide)

    copies = []
    for k, peer in enumerate(samp_peers):
        copy = remote(
            part_ref.at[rows_of(peer[0]), :],
            rows_in.at[k],
            sems_a.at[0, k],
            sems_a.at[1, k],
            peer,
        )
        copy.start()
        copies.append(copy)
    half[...] = part_ref[rows_of(me_s), :].astype(F32)
    for k, copy in enumerate(copies):
        copy.wait()
        half[...] += rows_in[k].astype(F32)
    copies = []
    for k, peer in enumerate(exp_peers):
        copy = remote(
            half.at[:, cols_of(peer[1])], cols_in.at[k], sems_b.at[0, k], sems_b.at[1, k], peer
        )
        copy.start()
        copies.append(copy)
    total = half[:, cols_of(me_g)]
    for k, copy in enumerate(copies):
        copy.wait()
        total = total + cols_in[k]
    final[...] = total.astype(BF16)
    out_ref[rows_of(me_s), cols_of(me_g)] = final[...]
    copies = []
    for k, peer in enumerate(exp_peers):
        copy = remote(
            final,
            out_ref.at[rows_of(me_s), cols_of(me_g)],
            sems_b.at[2, k],
            sems_b.at[3, k],
            peer,
        )
        copy.start()
        copies.append(copy)
    for copy in copies:
        copy.wait()
    copies = []
    for k, peer in enumerate(samp_peers):
        copy = remote(
            out_ref.at[rows_of(me_s), :],
            out_ref.at[rows_of(me_s), :],
            sems_a.at[2, k],
            sems_a.at[3, k],
            peer,
        )
        copy.start()
        copies.append(copy)
    for copy in copies:
        copy.wait()


def mix(part, ns, ng):
    tokens, width = part.shape
    high = tokens // ns
    return pl.pallas_call(
        functools.partial(mix_kernel, ns, ng),
        out_shape=jax.ShapeDtypeStruct(part.shape, BF16),
        in_specs=[VMEM],
        out_specs=VMEM,
        scratch_shapes=[
            pltpu.VMEM((ns - 1, high, width), BF16),
            pltpu.VMEM((high, width), F32),
            pltpu.VMEM((ng - 1, high, width // ng), F32),
            pltpu.VMEM((high, width // ng), BF16),
            pltpu.SemaphoreType.DMA((4, ns - 1)),
            pltpu.SemaphoreType.DMA((4, ng - 1)),
        ],
        compiler_params=pltpu.CompilerParams(collective_id=1, has_side_effects=True),
    )(part)


def total_kernel(ns, ng, mine_ref, out_ref, slots, sends, recvs):
    me = lax.axis_index("samp") * ng + lax.axis_index("exp")
    devices = ns * ng
    barrier = pltpu.get_barrier_semaphore()

    def peer_of(k):
        index = lax.rem(me + k, devices)
        return (index // ng, lax.rem(index, ng))

    def hello(k, carry):
        pl.semaphore_signal(barrier, inc=1, device_id=peer_of(k), device_id_type=MESH)
        return carry

    lax.fori_loop(1, devices, hello, 0)
    pl.semaphore_wait(barrier, devices - 1)

    def copy_of(k):
        return remote(mine_ref, slots.at[me], sends.at[k], recvs.at[k], peer_of(k))

    def send(k, carry):
        copy_of(k).start()
        return carry

    lax.fori_loop(1, devices, send, 0)
    slots[me] = mine_ref[...]

    def take(k, carry):
        copy_of(k).wait()
        return carry

    lax.fori_loop(1, devices, take, 0)
    out_ref[...] = jnp.sum(slots[...], axis=0)


def total_of(values, ns, ng):
    devices = ns * ng
    return pl.pallas_call(
        functools.partial(total_kernel, ns, ng),
        out_shape=jax.ShapeDtypeStruct(values.shape, F32),
        in_specs=[VMEM],
        out_specs=VMEM,
        scratch_shapes=[
            pltpu.VMEM((devices,) + values.shape, F32),
            pltpu.SemaphoreType.DMA((devices,)),
            pltpu.SemaphoreType.DMA((devices,)),
        ],
        compiler_params=pltpu.CompilerParams(collective_id=2, has_side_effects=True),
    )(values)


def per_device(
    prompt_states, edit_offsets, targets, router, route_ids, chosen, lengths, w_gate, w_up, w_down
):
    seq = prompt_states.shape[2]
    width = prompt_states.shape[3]
    rounds = route_ids.shape[0]
    top = route_ids.shape[4]
    experts = router.shape[1]
    cap = seq * top * 5 // (4 * experts)
    samplers = lax.axis_size("samp")
    groups = lax.axis_size("exp")
    my_samp = lax.axis_index("samp")
    my_group = lax.axis_index("exp")
    my_expert = my_samp * groups + my_group
    block = -(-groups * cap // 16) * 16
    rows = samplers * block
    tokens = groups * seq
    gate_weight, up_weight, down_weight = w_gate[0], w_up[0], w_down[0]
    meta_width = -(-(experts + 4) // 128) * 128
    expert_iota = jnp.arange(experts, dtype=jnp.int32)
    positions = jnp.arange(seq, dtype=jnp.int32)

    row_iota = jnp.arange(rows, dtype=jnp.int32)
    row_samp = row_iota // block
    row_group = jnp.minimum((row_iota % block) // cap, groups - 1)
    row_repair = row_samp * groups + row_group
    repair_onehot = row_repair[:, None] == jnp.arange(samplers * groups, dtype=jnp.int32)[None, :]
    token_iota = jnp.arange(tokens, dtype=jnp.int32)
    tril = (positions[:, None] <= positions[None, :]).astype(BF16)

    def meta_of(r):
        mask = jnp.any(route_ids[r, 0, 0][:, :, None] == expert_iota[None, None, :], axis=1)
        length = lengths[r, 0, 0]
        cols = jnp.stack(
            [
                positions.astype(BF16),
                (positions < length).astype(BF16),
                jnp.broadcast_to(length.astype(BF16), (seq,)),
                jnp.ones((seq,), BF16),
            ],
            axis=1,
        )
        pad = jnp.zeros((seq, meta_width - experts - 4), BF16)
        return jnp.concatenate([mask.astype(BF16), cols, pad], axis=1)

    def code_of(r):
        hit = metas[r][:, :experts]
        rank = dot_tn(hit, tril) - 1.0
        own = dot_tn(hit, jnp.eye(seq, dtype=BF16))
        code = jnp.where(own > 0.5, rank + (my_group * cap).astype(F32), -1.0)
        return code.reshape(samplers, groups, seq).transpose(1, 0, 2)

    def columns_of(meta):
        info = meta[:, experts : experts + 4].astype(F32)
        used = info[:, 3] > 0.5
        return meta[:, :experts] > 0.5, info[:, 0].astype(jnp.int32), info[:, 1], info[:, 2], used

    def gates_of(received, mask, used):
        logits = dot(received, router)
        sig = jnp.where(mask, jax.nn.sigmoid(logits), 0.0)
        total = jnp.where(used, jnp.sum(sig, axis=1), 1.0)
        own = jnp.sum(jnp.where(expert_iota[None, :] == my_expert, sig, 0.0), axis=1)
        return (own / total).astype(BF16)

    def own_part(x, target, r):
        length = lengths[r, 0, 0]
        valid = (positions < length).astype(F32)
        score = jnp.sum(x.astype(F32) * target.astype(F32), axis=1) / math.sqrt(width)
        return jnp.sum(valid * score) / length.astype(F32)

    def reward_part(hidden, back, gate, valid, length, used, own):
        score = jnp.sum(hidden.astype(F32) * back, axis=1) / math.sqrt(width)
        score = gate.astype(F32) * valid * score / jnp.where(used, length, 1.0)
        part = jnp.sum(jnp.where(repair_onehot, score[:, None], 0.0), axis=0)
        repairs = jnp.arange(samplers * groups, dtype=jnp.int32)
        return part + jnp.where(repairs == my_expert, own, 0.0)

    metas = [meta_of(r) for r in range(rounds)]
    bases = [prompt_states[0, 0]] + [edit_offsets[r, 0, 0] for r in range(rounds - 1)]
    arrays = []
    for r in range(rounds):
        arrays += [jnp.concatenate([bases[r], metas[r]], axis=1), targets[r, 0, 0]]
    code = jnp.concatenate([code_of(r) for r in range(rounds)], axis=2)
    landed = dispatch(code, arrays, samplers, groups, seq, block, rounds)
    parts = []
    saved = []
    mixed = None
    for r in range(rounds):
        arrived, target_rows = landed[2 * r], landed[2 * r + 1]
        mask, row_pos, valid, length, used = columns_of(arrived[:, width:])
        received = arrived[:, :width]
        token_code = jnp.where(used, row_group * seq + row_pos, -1)
        own_x = bases[r]
        if r > 0:
            lift = (token_code[:, None] == token_iota[None, :]).astype(BF16)
            received = (dot(lift, mixed) + received.astype(F32)).astype(BF16)
            best = lax.dynamic_slice_in_dim(mixed, my_group * seq, seq, axis=0)
            own_x = (best.astype(F32) + own_x.astype(F32)).astype(BF16)
        gate = gates_of(received, mask, used)
        pre_gate = dot(received, gate_weight)
        pre_up = dot(received, up_weight)
        hidden = (jax.nn.silu(pre_gate) * pre_up).astype(BF16)
        if r + 1 < rounds:
            choice = chosen[r]
            row_choice = jnp.sum(
                jnp.where(
                    row_group[:, None] == jnp.arange(groups, dtype=jnp.int32)[None, :],
                    choice[None, :],
                    0,
                ),
                axis=1,
            )
            keep = row_samp == row_choice
            slot_code = jnp.where(keep, row_iota % block, -1)
            slots = jnp.arange(block, dtype=jnp.int32)
            take = (slot_code[None, :] == slots[:, None]).astype(BF16)
            result = dot(dot(take, hidden).astype(BF16), down_weight).astype(BF16)
            spread = jnp.where(
                (jnp.where(keep, token_code, -1)[:, None] == token_iota[None, :]),
                gate[:, None],
                jnp.zeros((), BF16),
            )
            combine = dot(take, spread).astype(BF16)
            start = (choice[token_iota // seq] == my_samp) & (token_iota // seq == my_group)
            wide_x = jnp.tile(own_x, (groups, 1)).astype(F32)
            part = dot_tn(combine, result) + jnp.where(start[:, None], wide_x, 0.0)
            mixed = mix(part.astype(BF16), samplers, groups)
        back = dot_nt(target_rows, down_weight)
        parts.append(
            reward_part(
                hidden, back, gate, valid, length, used, own_part(own_x, targets[r, 0, 0], r)
            )
        )
        saved.append((received, target_rows, gate, valid, pre_gate, pre_up, hidden, back))
    filled = jnp.zeros((8, -(-samplers * groups // 128) * 128), F32)
    filled = filled.at[:rounds, : samplers * groups].set(jnp.stack(parts))
    rewards = total_of(filled, samplers, groups)[:rounds, : samplers * groups]
    rewards = rewards.reshape(rounds, samplers, groups)
    advantage = rewards - jnp.mean(rewards, axis=1, keepdims=True)
    flat = advantage.reshape(rounds, samplers * groups)
    grad_gate = grad_up = grad_down = 0.0
    for r, (received, target_rows, gate, valid, pre_gate, pre_up, hidden, back) in enumerate(saved):
        row_adv = jnp.sum(jnp.where(repair_onehot, flat[r][None, :], 0.0), axis=1)
        coef = (row_adv * valid * gate.astype(F32)).astype(BF16).astype(F32)[:, None]
        hidden_grad = coef * back
        sg = jax.nn.sigmoid(pre_gate)
        gate_grad = (hidden_grad * pre_up * sg * (1.0 + pre_gate * (1.0 - sg))).astype(BF16)
        up_grad = (hidden_grad * pre_gate * sg).astype(BF16)
        weighted = (hidden.astype(F32) * coef).astype(BF16)
        grad_down = grad_down + dot_tn(weighted, target_rows)
        grad_gate = grad_gate + dot_tn(received, gate_grad)
        grad_up = grad_up + dot_tn(received, up_grad)
    repairs = jnp.arange(samplers * groups, dtype=jnp.int32)
    my_adv = jnp.sum(jnp.where(repairs[None, :] == my_expert, flat, 0.0), axis=1)
    return (
        grad_gate.astype(BF16)[None],
        grad_up.astype(BF16)[None],
        grad_down.astype(BF16)[None],
        my_adv.reshape(rounds, 1, 1),
    )


def solution(mesh):
    placed = (
        P("exp", "samp", None, None),
        P(None, "exp", "samp", None, None),
        P(None, "exp", "samp", None, None),
        P(),
        P(None, "exp", "samp", None, None),
        P(),
        P(None, "exp", "samp"),
        P(("samp", "exp"), None, None),
        P(("samp", "exp"), None, None),
        P(("samp", "exp"), None, None),
    )
    return jax.shard_map(
        per_device,
        mesh=mesh,
        in_specs=placed,
        out_specs=(
            P(("samp", "exp"), None, None),
            P(("samp", "exp"), None, None),
            P(("samp", "exp"), None, None),
            P(None, "exp", "samp"),
        ),
        check_vma=False,
    )
```

profile of v0, /device:TPU:0, one launch (start us, length us, event | category | flops | bytes accessed | tf_op | source)
XLA Modules:
  0.0 316.8 jit_solution(6772741495428948188)
XLA Ops:
  1.3 1.6 fusion.138
  5.4 1.4 fusion.137
  6.8 2.5 compare_reduce_fusion
  9.9 0.6 multiply_add_fusion
  10.5 0.7 select_reduce_fusion.6
  11.8 0.7 slice_bitcast_fusion.3
  13.4 0.6 stack_broadcast_in_dim.6
  14.1 0.7 fusion.110
  14.7 1.2 fusion.109
  16.0 1.1 concatenate.12.refs_1_
  17.1 1.8 concatenate.13.refs_3_
  18.8 1.0 bitcast_convert_fusion
  19.9 1.1 slice_bitcast_fusion
  21.0 1.6 bitcast_select_fusion
  22.5 148.0 %shard_map.129 = (bf16[640,2176]{1,0:T(8,128)(2,1)}, bf16[640,2048]{1,0:T(8,128)(2,1)S(1)}, bf16[640,2176]{1,0:T(8,128)(2,1)}, bf16[640,2048]{1,0:T(8,128)(2,1)}) custom-call(f32[4,8,128]{2,1,0:T(8,128)S(1)} %pad_maximum_fusion.refs_0_, bf16[64,2176]{1,0:T(8,128)(2,1)S(1)} %concatenate.12.refs_1_, bf16[64,2048]{1,0:T(8,128)(2,1)S(1)} %get-tuple-element.43.refs_2_, ...), custom_call_target="tpu_custom_call" | custom-call | tf_op jit(solution)/shard_map/pallas_call | solution.py:120
  170.6 3.6 %select_reduce_fusion.5 = (f32[640]{0:T(1024)S(1)}, f32[640]{0:T(1024)S(1)}) fusion(pred[32]{0:T(512)(128)(4,1)S(1)} %copy-done.21, bf16[2048,32]{0,1:T(8,128)(2,1)S(1)} %copy-done.30, bf16[640,2176]{1,0:T(8,128)(2,1)} %get-tuple-element.20), kind=kOutput, calls=%fused_computation.142 | convolution fusion | flops 84048640 | bytes 2921504 | tf_op jit(solution)/shard_map/dot_general | solution.py:16
  175.4 1.0 convolution_convert_fusion.1
  176.4 1.0 slice_convert_fusion.2
  177.5 1.7 fusion.89
  179.2 2.2 fusion.12
  181.4 2.2 fusion.8
  183.6 3.8 %fusion.21 = (f32[640]{0:T(1024)S(1)}, bf16[640,768]{1,0:T(8,128)(2,1)S(1)}, f32[640,768]{1,0:T(8,128)}) fusion(f32[640,768]{1,0:T(8,128)S(1)} %fusion.8, f32[640,768]{1,0:T(8,128)S(1)} %fusion.12, bf16[640,2048]{1,0:T(8,128)(2,1)S(1)} %get-tuple-element.21, bf16[1,768,2048]{2,1,0:T(8,128)(2,1)S(1)} %copy-done), kind=kOutput, calls=%fused_computation.29 | convolution fusion | flops 2017688960 | bytes 12651008 | tf_op jit(solution)/shard_map/dot_general | solution.py:24
  187.5 1.2 fusion.101
  188.7 0.9 convolution_convert_fusion
  189.6 3.6 %fusion.17.part_ref = bf16[256,2048]{1,0:T(8,128)(2,1)} fusion(f32[256,2048]{1,0:T(8,128)} %bitcast_select_fusion, bf16[80,256]{1,0:T(8,128)(2,1)} %convolution_convert_fusion.1, bf16[80,768]{1,0:T(8,128)(2,1)} %convolution_convert_fusion, bf16[1,768,2048]{2,1,0:T(8,128)(2,1)S(1)} %copy-done), kind=kOutput, calls=%fused_computation.22 | convolution fusion | flops 336756736 | bytes 6455296 | tf_op jit(solution)/shard_map/dot_general | solution.py:20
  193.2 56.9 %shard_map.130 = bf16[256,2048]{1,0:T(8,128)(2,1)} custom-call(bf16[256,2048]{1,0:T(8,128)(2,1)} %fusion.17.part_ref), custom_call_target="tpu_custom_call" | custom-call | tf_op jit(solution)/shard_map/pallas_call | solution.py:215
  250.1 2.1 multiply_reduce_fusion.1
  252.2 1.3 fusion.129
  254.1 1.9 fusion.128
  256.6 3.0 add_convert_fusion.3
  259.7 2.4 select_reduce_fusion.3
  262.6 2.2 fusion.10
  264.8 2.2 fusion.6
  267.3 4.0 %fusion.23 = (f32[640]{0:T(1024)S(1)}, bf16[640,768]{1,0:T(8,128)(2,1)}, f32[640,768]{1,0:T(8,128)}) fusion(f32[640,768]{1,0:T(8,128)S(1)} %fusion.6, f32[640,768]{1,0:T(8,128)S(1)} %fusion.10, bf16[640,2048]{1,0:T(8,128)(2,1)S(1)} %copy-done.28, bf16[1,768,2048]{2,1,0:T(8,128)(2,1)S(1)} %copy-done), kind=kOutput, calls=%fused_computation.31 | convolution fusion | flops 2017688960 | bytes 12651008 | tf_op jit(solution)/shard_map/dot_general | solution.py:24
  271.3 0.6 fusion.100
  272.3 0.6 select_maximum_fusion.mine_ref
  272.9 11.4 %shard_map.131 = f32[8,128]{1,0:T(8,128)} custom-call(f32[8,128]{1,0:T(8,128)} %select_maximum_fusion.mine_ref), custom_call_target="tpu_custom_call" | custom-call | tf_op jit(solution)/shard_map/pallas_call | solution.py:268
  284.3 0.7 slice.121
  285.3 1.0 select_reduce_fusion
  286.3 1.2 convert_reduce_fusion.1
  287.5 1.5 convert_reduce_fusion
  289.1 1.3 select_reduce_fusion.7
  290.5 5.0 %fusion.59 = f32[768,2048]{1,0:T(8,128)S(1)} fusion(bf16[640,2048]{1,0:T(8,128)(2,1)} %copy-done.3, bf16[640,768]{1,0:T(8,128)(2,1)} %copy-done.8, f32[640]{0:T(1024)S(1)} %convert_reduce_fusion.1), kind=kOutput, calls=%fused_computation.69 | convolution fusion | flops 2014740480 | bytes 9898496 | tf_op jit(solution)/shard_map/dot_general | solution.py:20
  295.5 4.6 %fusion.16 = bf16[1,768,2048]{2,1,0:T(8,128)(2,1)} fusion(f32[768,2048]{1,0:T(8,128)S(1)} %fusion.59, bf16[640,2048]{1,0:T(8,128)(2,1)S(1)} %copy-done.29, bf16[640,768]{1,0:T(8,128)(2,1)S(1)} %copy-done.37, f32[640]{0:T(1024)S(1)} %convert_reduce_fusion), kind=kOutput, calls=%fused_computation.20 | convolution fusion | flops 2017886208 | bytes 13044224 | tf_op jit(solution)/shard_map/dot_general | solution.py:20
  300.1 3.0 fusion.27
  303.6 5.0 %fusion.14 = bf16[1,2048,768]{2,1,0:T(8,128)(2,1)} fusion(f32[2048,768]{1,0:T(8,128)S(1)} %fusion.27, bf16[640,2048]{1,0:T(8,128)(2,1)S(1)} %copy-done.7, f32[640,768]{1,0:T(8,128)S(1)} %copy-done.33, f32[640,768]{1,0:T(8,128)S(1)} %copy-done.36, f32[640,768]{1,0:T(8,128)S(1)} %copy-done.34, f32[640]{0:T(1024)S(1)} %convert_reduce_fusion), kind=kOutput, calls=%fused_computation.18 | convolution fusion | flops 2021818368 | bytes 17959424 | tf_op jit(solution)/shard_map/dot_general | solution.py:20
  308.7 3.0 fusion.25
  311.6 4.7 %fusion.15 = bf16[1,2048,768]{2,1,0:T(8,128)(2,1)} fusion(f32[2048,768]{1,0:T(8,128)S(1)} %fusion.25, bf16[640,2048]{1,0:T(8,128)(2,1)S(1)} %copy-done.7, f32[640,768]{1,0:T(8,128)S(1)} %copy-done.33, f32[640,768]{1,0:T(8,128)S(1)} %copy-done.34, f32[640]{0:T(1024)S(1)} %convert_reduce_fusion), kind=kOutput, calls=%fused_computation.19 | convolution fusion | flops 2019852288 | bytes 15993344 | tf_op jit(solution)/shard_map/dot_general | solution.py:20
  (123 shorter events, 5.8 us)
Async XLA Ops:
  0.6 183.0 %copy-start = (bf16[1,768,2048]{2,1,0:T(8,128)(2,1)S(1)}, bf16[1,768,2048]{2,1,0:T(8,128)(2,1)}, u32[]{:S(2)}) copy-start(bf16[1,768,2048]{2,1,0:T(8,128)(2,1)} %param.21) | copy-start | bytes 9437188
  11.2 1.8 copy-start.12
  17.1 3.9 %copy-start.23 = (pred[256]{0:T(512)(128)(4,1)S(1)}, pred[256]{0:T(512)(128)(4,1)}, u32[]{:S(2)}) copy-start(pred[256]{0:T(512)(128)(4,1)} %compare_and_fusion) | copy-start | bytes 772
  18.8 3.7 %copy-start.2 = (bf16[64,2176]{1,0:T(8,128)(2,1)S(1)}, bf16[64,2176]{1,0:T(8,128)(2,1)}, u32[]{:S(2)}) copy-start(bf16[64,2176]{1,0:T(8,128)(2,1)} %concatenate.13.refs_3_) | copy-start | bytes 835588
  20.9 149.6 %copy-start.21 = (pred[32]{0:T(512)(128)(4,1)S(1)}, pred[32]{0:T(512)(128)(4,1)}, u32[]{:S(2)}) copy-start(pred[32]{0:T(512)(128)(4,1)} %iota_compare_fusion.20) | copy-start | bytes 100
  20.9 149.6 %copy-start.30 = (bf16[2048,32]{0,1:T(8,128)(2,1)S(1)}, bf16[2048,32]{0,1:T(8,128)(2,1)}, u32[]{:S(2)}) copy-start(bf16[2048,32]{0,1:T(8,128)(2,1)} %param.15) | copy-start | bytes 393220
  170.6 13.0 %copy-start.3 = (bf16[640,2048]{1,0:T(8,128)(2,1)}, bf16[640,2048]{1,0:T(8,128)(2,1)S(1)}, u32[]{:S(2)}) copy-start(bf16[640,2048]{1,0:T(8,128)(2,1)S(1)} %get-tuple-element.21) | copy-start | bytes 7864324
  170.6 3.7 %copy-start.19 = (bf16[640,2176]{1,0:T(8,128)(2,1)S(1)}, bf16[640,2176]{1,0:T(8,128)(2,1)}, u32[]{:S(2)}) copy-start(bf16[640,2176]{1,0:T(8,128)(2,1)} %get-tuple-element.20) | copy-start | bytes 8355844
  170.6 4.3 %copy-start.13 = (s32[640]{0:T(1024)S(1)}, s32[640]{0:T(1024)}, u32[]{:S(2)}) copy-start(s32[640]{0:T(1024)} %copy-done.12) | copy-start | bytes 7684
  170.6 4.8 %copy-start.15 = (s32[640]{0:T(1024)S(1)}, s32[640]{0:T(1024)}, u32[]{:S(2)}) copy-start(s32[640]{0:T(1024)} %fusion.118) | copy-start | bytes 7684
  174.3 13.2 %copy-start.10 = (f32[640]{0:T(1024)}, f32[640]{0:T(1024)S(1)}, u32[]{:S(2)}) copy-start(f32[640]{0:T(1024)S(1)} %get-tuple-element.28) | copy-start | bytes 7684
  174.3 13.2 %copy-start.11 = (f32[640]{0:T(1024)}, f32[640]{0:T(1024)S(1)}, u32[]{:S(2)}) copy-start(f32[640]{0:T(1024)S(1)} %get-tuple-element.29) | copy-start | bytes 7684
  174.3 4.9 %copy-start.24 = (bf16[1,2048,768]{2,1,0:T(8,128)(2,1)S(1)}, bf16[1,2048,768]{2,1,0:T(8,128)(2,1)}, u32[]{:S(2)}) copy-start(bf16[1,2048,768]{2,1,0:T(8,128)(2,1)} %param.19) | copy-start | bytes 9437188
  177.5 3.9 %copy-start.4 = (f32[640,4]{1,0:T(8,128)}, f32[640,4]{1,0:T(8,128)S(1)}, u32[]{:S(2)}) copy-start(f32[640,4]{1,0:T(8,128)S(1)} %slice_convert_fusion.2) | copy-start | bytes 30724
  179.2 2.2 copy-start.26
  181.4 2.2 copy-start.38
  183.6 3.8 %copy-start.40 = (f32[640,768]{1,0:T(8,128)}, f32[640,768]{1,0:T(8,128)S(1)}, u32[]{:S(2)}) copy-start(f32[640,768]{1,0:T(8,128)S(1)} %fusion.8) | copy-start | bytes 5898244
  187.4 1.2 copy-start.8
  256.6 3.0 copy-start.22
  256.6 3.0 copy-start.31
  259.6 5.2 %copy-start.6 = (bf16[640,2048]{1,0:T(8,128)(2,1)}, bf16[640,2048]{1,0:T(8,128)(2,1)S(1)}, u32[]{:S(2)}) copy-start(bf16[640,2048]{1,0:T(8,128)(2,1)S(1)} %add_convert_fusion.3) | copy-start | bytes 7864324
  259.7 2.9 copy-start.25
  262.1 9.2 %copy-start.17 = (f32[640]{0:T(1024)}, f32[640]{0:T(1024)S(1)}, u32[]{:S(2)}) copy-start(f32[640]{0:T(1024)S(1)} %get-tuple-element.26) | copy-start | bytes 7684
  262.1 9.2 %copy-start.18 = (f32[640]{0:T(1024)}, f32[640]{0:T(1024)S(1)}, u32[]{:S(2)}) copy-start(f32[640]{0:T(1024)S(1)} %get-tuple-element.27) | copy-start | bytes 7684
  262.6 2.2 copy-start.27
  264.8 2.3 copy-start.32
  264.8 2.5 copy-start.28
  267.3 4.0 %copy-start.35 = (f32[640,768]{1,0:T(8,128)}, f32[640,768]{1,0:T(8,128)S(1)}, u32[]{:S(2)}) copy-start(f32[640,768]{1,0:T(8,128)S(1)} %fusion.6) | copy-start | bytes 5898244
  267.3 4.0 %copy-start.5 = (f32[640,4]{1,0:T(8,128)S(1)}, f32[640,4]{1,0:T(8,128)}, u32[]{:S(2)}) copy-start(f32[640,4]{1,0:T(8,128)} %copy-done.4) | copy-start | bytes 30724
  267.3 4.0 %copy-start.9 = (pred[640,1]{1,0:T(8,128)(4,1)S(1)}, pred[640,1]{1,0:T(8,128)(4,1)}, u32[]{:S(2)}) copy-start(pred[640,1]{1,0:T(8,128)(4,1)} %get-tuple-element.37) | copy-start | bytes 1924
  267.3 4.6 %copy-start.14 = (s32[640]{0:T(1024)S(1)}, s32[640]{0:T(1024)}, u32[]{:S(2)}) copy-start(s32[640]{0:T(1024)} %multiply_add_fusion) | copy-start | bytes 7684
  267.3 4.6 %copy-start.16 = (f32[640]{0:T(1024)S(1)}, f32[640]{0:T(1024)}, u32[]{:S(2)}) copy-start(f32[640]{0:T(1024)} %fusion.101) | copy-start | bytes 7684
  290.5 5.0 %copy-start.29 = (bf16[640,2048]{1,0:T(8,128)(2,1)S(1)}, bf16[640,2048]{1,0:T(8,128)(2,1)}, u32[]{:S(2)}) copy-start(bf16[640,2048]{1,0:T(8,128)(2,1)} %get-tuple-element.23) | copy-start | bytes 7864324
  290.5 5.0 %copy-start.37 = (bf16[640,768]{1,0:T(8,128)(2,1)S(1)}, bf16[640,768]{1,0:T(8,128)(2,1)}, u32[]{:S(2)}) copy-start(bf16[640,768]{1,0:T(8,128)(2,1)} %get-tuple-element.35) | copy-start | bytes 2949124
  295.4 4.6 %copy-start.20 = (bf16[640,2176]{1,0:T(8,128)(2,1)S(1)}, bf16[640,2176]{1,0:T(8,128)(2,1)}, u32[]{:S(2)}) copy-start(bf16[640,2176]{1,0:T(8,128)(2,1)} %get-tuple-element.20) | copy-start | bytes 8355844
  295.5 4.6 %copy-start.39 = (f32[640,768]{1,0:T(8,128)S(1)}, f32[640,768]{1,0:T(8,128)}, u32[]{:S(2)}) copy-start(f32[640,768]{1,0:T(8,128)} %copy-done.38) | copy-start | bytes 5898244
  295.5 4.6 %copy-start.41 = (f32[640,768]{1,0:T(8,128)S(1)}, f32[640,768]{1,0:T(8,128)}, u32[]{:S(2)}) copy-start(f32[640,768]{1,0:T(8,128)} %copy-done.40) | copy-start | bytes 5898244
  295.5 4.6 %copy-start.42 = (f32[640,768]{1,0:T(8,128)S(1)}, f32[640,768]{1,0:T(8,128)}, u32[]{:S(2)}) copy-start(f32[640,768]{1,0:T(8,128)} %get-tuple-element.54) | copy-start | bytes 5898244
  300.1 3.1 copy-start.7
  300.1 3.1 copy-start.33
  300.1 3.1 copy-start.34
  300.1 3.5 %copy-start.36 = (f32[640,768]{1,0:T(8,128)S(1)}, f32[640,768]{1,0:T(8,128)}, u32[]{:S(2)}) copy-start(f32[640,768]{1,0:T(8,128)} %copy-done.35) | copy-start | bytes 5898244
  311.6 4.7 %copy-start.1 = (bf16[1,768,2048]{2,1,0:T(8,128)(2,1)S(1)}, bf16[1,768,2048]{2,1,0:T(8,128)(2,1)}, u32[]{:S(2)}) copy-start(bf16[1,768,2048]{2,1,0:T(8,128)(2,1)} %param.21) | copy-start | bytes 9437188
where the time goes:
time: 321 us; the launch traced here: 317 us
  Pallas kernels  216 us (67%)
  matrix products  57 us (18%)
  other arithmetic  27.2 us (8%)
  local copies, waits for them, and re-layouts  10.7 us (3%)
  between operations  5.68 us (2%)
    pallas_call x1, Pallas kernels, dispatch(): pl.pallas_call(functools.partial(dispatch_kernel, ns, ng, seq, block, rou...  148 us
    pallas_call x1, Pallas kernels, mix(): pl.pallas_call(functools.partial(mix_kernel, ns, ng), out_shape=jax.Shape...  56.9 us
    dot_general x11, matrix products, dot_tn(): lax.dot_general(a, b, (((0,), (0,)), ((), ())), preferred_element_type=F32)  29.4 us
    dot_general x9, matrix products, dot(): return jnp.dot(a, b, preferred_element_type=F32)  19.8 us
    pallas_call x1, Pallas kernels, total_of(): pl.pallas_call(functools.partial(total_kernel, ns, ng), out_shape=jax.Sha...  11.4 us
    dot_general x2, matrix products, dot_nt(): lax.dot_general(a, b, (((1,), (1,)), ((), ())), preferred_element_type=F32)  7.77 us

commit v1 on v0

--- a/solution.py
+++ b/solution.py
@@ -42,35 +42,40 @@
     )
 
 
-def dispatch_kernel(ns, ng, seq, block, rounds, *refs):
+def dispatch_kernel(ns, ng, seq, block, rounds, chunks, *refs):
     count = 2 * rounds
-    code_ref, ins, outs = refs[0], refs[1 : 1 + count], refs[1 + count : 1 + 2 * count]
-    rest = refs[1 + 2 * count :]
-    codes, alls, sends = rest[0], rest[1 : 1 + count], rest[1 + count : 1 + 2 * count]
-    place, gs, gr, ss, sr, own_sem = rest[1 + 2 * count :]
+    code_ref, meta_ref, target_ref = refs[:3]
+    bases = refs[3 : 3 + rounds]
+    outs, rest = refs[3 + rounds : 3 + rounds + count], refs[3 + rounds + count :]
+    codes, alls, sends = rest[0], rest[1 : 1 + count], list(rest[1 + count : count * 2]) + [outs[-1]]
+    place, gs, gr, ss, sr, own_sem = rest[count * 2 :]
+    width = bases[0].shape[1]
     me_s, me_g = lax.axis_index("samp"), lax.axis_index("exp")
     exp_peers = [(me_s, lax.rem(me_g + k, ng)) for k in range(1, ng)]
     samp_peers = [(lax.rem(me_s + k, ns), me_g) for k in range(1, ns)]
+    mine = pl.ds(pl.multiple_of(me_g * seq, seq), seq)
+    codes[me_g] = code_ref[me_g]
+    for r in range(rounds):
+        alls[r][mine, :width] = bases[r][...]
+        alls[r][mine, width:] = meta_ref[r]
+        alls[rounds + r][mine, :] = target_ref[r]
     greet(exp_peers + samp_peers)
-    mine = pl.ds(pl.multiple_of(me_g * seq, seq), seq)
+
+    def gather(j):
+        i, lo, hi = chunks[j]
+        part = alls[i].at[mine, lo:hi]
+        here = [remote(part, part, gs.at[j, k], gr.at[j, k], p) for k, p in enumerate(exp_peers)]
+        for copy in here:
+            copy.start()
+        return here
+
     code_copies = []
     for k, peer in enumerate(exp_peers):
-        copy = remote(
-            code_ref.at[peer[1]], codes.at[me_g], gs.at[count, k], gr.at[count, k], peer
-        )
+        at = len(chunks)
+        copy = remote(code_ref.at[peer[1]], codes.at[me_g], gs.at[at, k], gr.at[at, k], peer)
         copy.start()
         code_copies.append(copy)
-    copies = []
-    for i in range(count):
-        here = []
-        for k, peer in enumerate(exp_peers):
-            copy = remote(ins[i], alls[i].at[mine, :], gs.at[i, k], gr.at[i, k], peer)
-            copy.start()
-            here.append(copy)
-        copies.append(here)
-    codes[me_g] = code_ref[me_g]
-    for i in range(count):
-        alls[i][mine, :] = ins[i][...]
+    flying = gather(0)
     for copy in code_copies:
         copy.wait()
     slots = lax.broadcasted_iota(jnp.int32, (block, ng * seq), 0).astype(F32)
@@ -80,66 +85,87 @@
             hit = jnp.where(line[d : d + 1, :] == slots, 1.0, 0.0)
             place[r, d * block : (d + 1) * block, :] = hit.astype(BF16)
     home = pl.ds(pl.multiple_of(me_s * block, block), block)
-    for i in range(count):
-        for copy in copies[i]:
+
+    def rows_of(d):
+        return pl.ds(pl.multiple_of(d * block, block), block)
+
+    def plane_copy(j, k):
+        i, lo, hi = chunks[j]
+        d = lax.rem(me_s + k, ns)
+        src, dst = sends[i].at[rows_of(d), lo:hi], outs[i].at[home, lo:hi]
+        return remote(src, dst, ss.at[j, k], sr.at[j, k], (d, me_g))
+
+    def home_copy(j):
+        i, lo, hi = chunks[j]
+        return pltpu.make_async_copy(
+            sends[i].at[home, lo:hi], outs[i].at[home, lo:hi], own_sem.at[j]
+        )
+
+    for j, (i, lo, hi) in enumerate(chunks):
+        for copy in flying:
             copy.wait()
-
-        def put(d, i=i):
-            part = pl.ds(pl.multiple_of(d * block, block), block)
-            sends[i][part, :] = dot(place[i // 2, part, :], alls[i][...]).astype(BF16)
-            return part
-
-        def step(k, carry, i=i, put=put):
+        if j + 1 < len(chunks):
+            flying = gather(j + 1)
+        held = i == count - 1
+
+        def step(k, carry, j=j, i=i, lo=lo, hi=hi, held=held):
             d = lax.rem(me_s + k, ns)
-            part = put(d)
-            remote(
-                sends[i].at[part, :], outs[i].at[home, :], ss.at[i, k], sr.at[i, k], (d, me_g)
-            ).start()
+            placed = dot(place[i % rounds, rows_of(d), :], alls[i][:, lo:hi])
+            sends[i][rows_of(d), lo:hi] = placed.astype(BF16)
+            if not held:
+                plane_copy(j, k).start()
             return carry
 
         lax.fori_loop(1, ns, step, 0)
-        put(me_s)
-        pltpu.make_async_copy(sends[i].at[home, :], outs[i].at[home, :], own_sem.at[i]).start()
-    for i in range(count):
-
-        def finish(k, carry, i=i):
-            d = lax.rem(me_s + k, ns)
-            part = pl.ds(pl.multiple_of(d * block, block), block)
-            remote(
-                sends[i].at[part, :], outs[i].at[home, :], ss.at[i, k], sr.at[i, k], (d, me_g)
-            ).wait()
+        placed = dot(place[i % rounds, home, :], alls[i][:, lo:hi])
+        sends[i][home, lo:hi] = placed.astype(BF16)
+        if not held:
+            home_copy(j).start()
+    for j, (i, lo, hi) in enumerate(chunks):
+        if i == count - 1:
+            continue
+
+        def finish(k, carry, j=j):
+            plane_copy(j, k).wait()
             return carry
 
         lax.fori_loop(1, ns, finish, 0)
-        pltpu.make_async_copy(sends[i].at[home, :], outs[i].at[home, :], own_sem.at[i]).wait()
-
-
-def dispatch(code, arrays, ns, ng, seq, block, rounds):
-    count = len(arrays)
-    widths = [a.shape[1] for a in arrays]
+        home_copy(j).wait()
+
+
+def dispatch(code, metas, targets, bases, ns, ng, seq, block, rounds):
+    width, extra = bases[0].shape[1], metas.shape[2]
+    widths = [width + extra] * rounds + [width] * rounds
+    half = width // 2
+    chunks = [(0, 0, half), (0, half, widths[0])] + [
+        (i, 0, widths[i]) for i in range(1, 2 * rounds)
+    ]
+    steps = len(chunks)
     return pl.pallas_call(
-        functools.partial(dispatch_kernel, ns, ng, seq, block, rounds),
+        functools.partial(dispatch_kernel, ns, ng, seq, block, rounds, chunks),
         out_shape=[jax.ShapeDtypeStruct((ns * block, w), BF16) for w in widths],
-        in_specs=[VMEM] * (1 + count),
-        out_specs=[ANY] * count,
+        in_specs=[VMEM] * (3 + rounds),
+        out_specs=[ANY] * (2 * rounds - 1) + [VMEM],
         scratch_shapes=[pltpu.VMEM(code.shape, F32)]
         + [pltpu.VMEM((ng * seq, w), BF16) for w in widths]
-        + [pltpu.VMEM((ns * block, w), BF16) for w in widths]
+        + [pltpu.VMEM((ns * block, w), BF16) for w in widths[:-1]]
         + [
             pltpu.VMEM((rounds, ns * block, ng * seq), BF16),
-            pltpu.SemaphoreType.DMA((count + 1, ng - 1)),
-            pltpu.SemaphoreType.DMA((count + 1, ng - 1)),
-            pltpu.SemaphoreType.DMA((count, ns)),
-            pltpu.SemaphoreType.DMA((count, ns)),
-            pltpu.SemaphoreType.DMA((count,)),
+            pltpu.SemaphoreType.DMA((steps + 1, ng - 1)),
+            pltpu.SemaphoreType.DMA((steps + 1, ng - 1)),
+            pltpu.SemaphoreType.DMA((steps, ns)),
+            pltpu.SemaphoreType.DMA((steps, ns)),
+            pltpu.SemaphoreType.DMA((steps,)),
         ],
         compiler_params=pltpu.CompilerParams(
             collective_id=0, has_side_effects=True, vmem_limit_bytes=48 * 2**20
         ),
-    )(code, *arrays)
-
-
-def mix_kernel(ns, ng, part_ref, out_ref, rows_in, half, cols_in, final, sems_a, sems_b):
+    )(code, metas, targets, *bases)
+
+
+def mix_kernel(
+    ns, ng, part_ref, ahead_ref, out_ref, landed_ref, rows_in, half, cols_in, final, sems_a, sems_b, own
+):
     me_s, me_g = lax.axis_index("samp"), lax.axis_index("exp")
     exp_peers = [(me_s, lax.rem(me_g + k, ng)) for k in range(1, ng)]
     samp_peers = [(lax.rem(me_s + k, ns), me_g) for k in range(1, ns)]
@@ -168,6 +194,26 @@
     for k, copy in enumerate(copies):
         copy.wait()
         half[...] += rows_in[k].astype(F32)
+    block = ahead_ref.shape[0] // ns
+
+    def block_of(d):
+        return pl.ds(pl.multiple_of(d * block, block), block)
+
+    ahead = [
+        remote(
+            ahead_ref.at[block_of(peer[0]), :],
+            landed_ref.at[block_of(me_s), :],
+            sems_a.at[4, k],
+            sems_a.at[5, k],
+            peer,
+        )
+        for k, peer in enumerate(samp_peers)
+    ]
+    ahead.append(
+        pltpu.make_async_copy(
+            ahead_ref.at[block_of(me_s), :], landed_ref.at[block_of(me_s), :], own
+        )
+    )
     copies = []
     for k, peer in enumerate(exp_peers):
         copy = remote(
@@ -175,6 +221,8 @@
         )
         copy.start()
         copies.append(copy)
+    for copy in ahead:
+        copy.start()
     total = half[:, cols_of(me_g)]
     for k, copy in enumerate(copies):
         copy.wait()
@@ -205,28 +253,32 @@
         )
         copy.start()
         copies.append(copy)
-    for copy in copies:
+    for copy in copies + ahead:
         copy.wait()
 
 
-def mix(part, ns, ng):
+def mix(part, ahead, ns, ng):
     tokens, width = part.shape
     high = tokens // ns
     return pl.pallas_call(
         functools.partial(mix_kernel, ns, ng),
-        out_shape=jax.ShapeDtypeStruct(part.shape, BF16),
-        in_specs=[VMEM],
-        out_specs=VMEM,
+        out_shape=[
+            jax.ShapeDtypeStruct(part.shape, BF16),
+            jax.ShapeDtypeStruct(ahead.shape, BF16),
+        ],
+        in_specs=[VMEM, ANY],
+        out_specs=[VMEM, ANY],
         scratch_shapes=[
             pltpu.VMEM((ns - 1, high, width), BF16),
             pltpu.VMEM((high, width), F32),
             pltpu.VMEM((ng - 1, high, width // ng), F32),
             pltpu.VMEM((high, width // ng), BF16),
-            pltpu.SemaphoreType.DMA((4, ns - 1)),
+            pltpu.SemaphoreType.DMA((6, ns - 1)),
             pltpu.SemaphoreType.DMA((4, ng - 1)),
+            pltpu.SemaphoreType.DMA,
         ],
         compiler_params=pltpu.CompilerParams(collective_id=1, has_side_effects=True),
-    )(part)
+    )(part, ahead)
 
 
 def total_kernel(ns, ng, mine_ref, out_ref, slots, sends, recvs):
@@ -358,16 +410,17 @@
 
     metas = [meta_of(r) for r in range(rounds)]
     bases = [prompt_states[0, 0]] + [edit_offsets[r, 0, 0] for r in range(rounds - 1)]
-    arrays = []
-    for r in range(rounds):
-        arrays += [jnp.concatenate([bases[r], metas[r]], axis=1), targets[r, 0, 0]]
     code = jnp.concatenate([code_of(r) for r in range(rounds)], axis=2)
-    landed = dispatch(code, arrays, samplers, groups, seq, block, rounds)
+    landed = list(
+        dispatch(
+            code, jnp.stack(metas), targets[:, 0, 0], bases, samplers, groups, seq, block, rounds
+        )
+    )
     parts = []
     saved = []
     mixed = None
     for r in range(rounds):
-        arrived, target_rows = landed[2 * r], landed[2 * r + 1]
+        arrived, target_rows = landed[r], landed[rounds + r]
         mask, row_pos, valid, length, used = columns_of(arrived[:, width:])
         received = arrived[:, :width]
         token_code = jnp.where(used, row_group * seq + row_pos, -1)
@@ -405,7 +458,7 @@
             start = (choice[token_iota // seq] == my_samp) & (token_iota // seq == my_group)
             wide_x = jnp.tile(own_x, (groups, 1)).astype(F32)
             part = dot_tn(combine, result) + jnp.where(start[:, None], wide_x, 0.0)
-            mixed = mix(part.astype(BF16), samplers, groups)
+            mixed, landed[-1] = mix(part.astype(BF16), landed[-1], samplers, groups)
         back = dot_nt(target_rows, down_weight)
         parts.append(
             reward_part(

time: 321 us -> 287 us (0.89)
  Pallas kernels: 216 us -> 189 us
  local copies, waits for them, and re-layouts: 10.7 us -> 7.01 us
    pallas_call x1, Pallas kernels: 148 us -> 110 us  [dispatch(): pl.pallas_call(functools.partial(dispatch_kernel, ns, ng, seq, block, rou...]
    pallas_call x1, Pallas kernels: 56.9 us -> 67.6 us  [mix(): pl.pallas_call(functools.partial(mix_kernel, ns, ng), out_shape=[jax.Shap...]
where the time goes in v1:
time: 287 us; the launch traced here: 284 us
  Pallas kernels  189 us (66%)
  matrix products  56.2 us (20%)
  other arithmetic  26.1 us (9%)
  local copies, waits for them, and re-layouts  7.01 us (2%)
  between operations  5.78 us (2%)
    pallas_call x1, Pallas kernels, dispatch(): pl.pallas_call(functools.partial(dispatch_kernel, ns, ng, seq, block, rou...  110 us
    pallas_call x1, Pallas kernels, mix(): pl.pallas_call(functools.partial(mix_kernel, ns, ng), out_shape=[jax.Shap...  67.6 us
    dot_general x11, matrix products, dot_tn(): lax.dot_general(a, b, (((0,), (0,)), ((), ())), preferred_element_type=F32)  29.4 us
    dot_general x9, matrix products, dot(): return jnp.dot(a, b, preferred_element_type=F32)  19.1 us
    pallas_call x1, Pallas kernels, total_of(): pl.pallas_call(functools.partial(total_kernel, ns, ng), out_shape=jax.Sha...  11.2 us
    dot_general x2, matrix products, dot_nt(): lax.dot_general(a, b, (((1,), (1,)), ((), ())), preferred_element_type=F32)  7.72 us

profile of v1, /device:TPU:0, one launch (start us, length us, event | category | flops | bytes accessed | tf_op | source)
XLA Modules:
  0.0 283.9 jit_solution(13397215600381496390)
XLA Ops:
  0.7 0.6 iota_compare_fusion.20
  1.3 1.6 fusion.140
  5.4 1.4 fusion.139
  6.8 2.5 compare_reduce_fusion
  9.9 0.6 multiply_add_fusion
  10.5 0.7 select_reduce_fusion.6
  11.2 0.6 fusion.120
  11.9 0.7 slice_bitcast_fusion.1
  13.5 0.7 fusion.111
  14.2 0.7 concatenate.12
  14.9 0.6 fusion.112
  15.7 0.8 pad_maximum_fusion.refs_1_
  16.5 1.0 bitcast_convert_fusion
  17.5 2.2 bitcast_select_fusion
  19.7 109.9 %shard_map.129 = (bf16[640,2176]{1,0:T(8,128)(2,1)}, bf16[640,2176]{1,0:T(8,128)(2,1)}, bf16[640,2048]{1,0:T(8,128)(2,1)S(1)}, bf16[640,2048]{1,0:T(8,128)(2,1)}) custom-call(f32[4,8,128]{2,1,0:T(8,128)S(1)} %pad_maximum_fusion.1.refs_0_, bf16[2,64,128]{2,1,0:T(8,128)(2,1)S(1)} %pad_maximum_fusion.refs_1_, bf16[2,64,2048]{2,1,0:T(8,128)(2,1)S(1)} %bitcast.91, ...), custom_call_target="tpu_custom_call" | custom-call | tf_op jit(solution)/shard_map/pallas_call | solution.py:144
  129.6 3.6 %select_reduce_fusion.5 = (f32[640]{0:T(1024)S(1)}, f32[640]{0:T(1024)S(1)}) fusion(pred[32]{0:T(512)(128)(4,1)S(1)} %copy-done.25, bf16[2048,32]{0,1:T(8,128)(2,1)S(1)} %copy-done.33, bf16[640,2176]{1,0:T(8,128)(2,1)} %get-tuple-element.22), kind=kOutput, calls=%fused_computation.144 | convolution fusion | flops 84048640 | bytes 2921504 | tf_op jit(solution)/shard_map/dot_general | solution.py:16
  133.9 0.5 fusion.88
  134.8 1.0 slice_convert_fusion.2
  135.9 1.1 fusion.91
  137.0 2.2 fusion.12
  139.2 2.2 fusion.8
  141.4 3.8 %fusion.21 = (f32[640]{0:T(1024)S(1)}, bf16[640,768]{1,0:T(8,128)(2,1)S(1)}, f32[640,768]{1,0:T(8,128)}) fusion(f32[640,768]{1,0:T(8,128)S(1)} %fusion.8, f32[640,768]{1,0:T(8,128)S(1)} %fusion.12, bf16[640,2048]{1,0:T(8,128)(2,1)S(1)} %get-tuple-element.23, bf16[1,768,2048]{2,1,0:T(8,128)(2,1)S(1)} %copy-done), kind=kOutput, calls=%fused_computation.29 | convolution fusion | flops 2017688960 | bytes 12651008 | tf_op jit(solution)/shard_map/dot_general | solution.py:24
  145.2 1.2 fusion.103
  146.4 0.9 convolution_convert_fusion
  147.4 3.6 %fusion.17.part_ref = bf16[256,2048]{1,0:T(8,128)(2,1)} fusion(f32[256,2048]{1,0:T(8,128)} %bitcast_select_fusion, bf16[80,256]{1,0:T(8,128)(2,1)S(1)} %convolution_convert_fusion.1, bf16[80,768]{1,0:T(8,128)(2,1)} %convolution_convert_fusion, bf16[1,768,2048]{2,1,0:T(8,128)(2,1)S(1)} %copy-done), kind=kOutput, calls=%fused_computation.22 | convolution fusion | flops 336756736 | bytes 6455296 | tf_op jit(solution)/shard_map/dot_general | solution.py:20
  151.0 67.6 %shard_map.130 = (bf16[256,2048]{1,0:T(8,128)(2,1)}, bf16[640,2048]{1,0:T(8,128)(2,1)}) custom-call(bf16[256,2048]{1,0:T(8,128)(2,1)} %fusion.17.part_ref, bf16[640,2048]{1,0:T(8,128)(2,1)} %get-tuple-element.25.ahead_ref), custom_call_target="tpu_custom_call" | custom-call | tf_op jit(solution)/shard_map/pallas_call | solution.py:263
  218.6 1.5 fusion.73
  220.1 1.2 fusion.131
  222.0 1.2 fusion.130
  223.9 3.0 %add_convert_fusion.3 = bf16[640,2048]{1,0:T(8,128)(2,1)S(1)} fusion(bf16[256,2048]{1,0:T(8,128)(2,1)} %get-tuple-element.26, bf16[640,2176]{1,0:T(8,128)(2,1)} %get-tuple-element.24, s32[640]{0:T(1024)S(1)} %get-tuple-element.40), kind=kOutput, calls=%fused_computation.3 | convolution fusion | flops 675184640 | bytes 6294016 | tf_op jit(solution)/shard_map/dot_general | solution.py:16
  226.9 2.4 select_reduce_fusion.3
  229.8 2.2 fusion.10
  232.1 2.2 fusion.6
  234.5 4.0 %fusion.23 = (f32[640]{0:T(1024)S(1)}, bf16[640,768]{1,0:T(8,128)(2,1)}, f32[640,768]{1,0:T(8,128)}) fusion(f32[640,768]{1,0:T(8,128)S(1)} %fusion.6, f32[640,768]{1,0:T(8,128)S(1)} %fusion.10, bf16[640,2048]{1,0:T(8,128)(2,1)S(1)} %copy-done.31, bf16[1,768,2048]{2,1,0:T(8,128)(2,1)S(1)} %copy-done), kind=kOutput, calls=%fused_computation.31 | convolution fusion | flops 2017688960 | bytes 12651008 | tf_op jit(solution)/shard_map/dot_general | solution.py:24
  238.5 0.6 fusion.102
  239.5 0.6 select_maximum_fusion.mine_ref
  240.1 11.2 %shard_map.131 = f32[8,128]{1,0:T(8,128)} custom-call(f32[8,128]{1,0:T(8,128)} %select_maximum_fusion.mine_ref), custom_call_target="tpu_custom_call" | custom-call | tf_op jit(solution)/shard_map/pallas_call | solution.py:320
  251.3 0.7 slice.119
  252.3 1.0 select_reduce_fusion
  253.4 1.2 convert_reduce_fusion.1
  254.6 1.5 convert_reduce_fusion
  256.2 1.3 select_reduce_fusion.7
  257.5 5.0 %fusion.59 = f32[768,2048]{1,0:T(8,128)S(1)} fusion(bf16[640,2048]{1,0:T(8,128)(2,1)} %copy-done.5, bf16[640,768]{1,0:T(8,128)(2,1)} %copy-done.12, f32[640]{0:T(1024)S(1)} %convert_reduce_fusion.1), kind=kOutput, calls=%fused_computation.69 | convolution fusion | flops 2014740480 | bytes 9898496 | tf_op jit(solution)/shard_map/dot_general | solution.py:20
  262.6 4.6 %fusion.16 = bf16[1,768,2048]{2,1,0:T(8,128)(2,1)} fusion(f32[768,2048]{1,0:T(8,128)S(1)} %fusion.59, bf16[640,2048]{1,0:T(8,128)(2,1)S(1)} %copy-done.32, bf16[640,768]{1,0:T(8,128)(2,1)S(1)} %copy-done.40, f32[640]{0:T(1024)S(1)} %convert_reduce_fusion), kind=kOutput, calls=%fused_computation.20 | convolution fusion | flops 2017886208 | bytes 13044224 | tf_op jit(solution)/shard_map/dot_general | solution.py:20
  267.2 3.0 %fusion.27 = f32[2048,768]{1,0:T(8,128)S(1)} fusion(bf16[640,2176]{1,0:T(8,128)(2,1)S(1)} %copy-done.24, f32[640,768]{1,0:T(8,128)S(1)} %copy-done.42, f32[640,768]{1,0:T(8,128)S(1)} %copy-done.44, f32[640,768]{1,0:T(8,128)S(1)} %copy-done.45, f32[640]{0:T(1024)S(1)} %convert_reduce_fusion.1), kind=kOutput, calls=%fused_computation.43 | convolution fusion | flops 2018672640 | bytes 14815232 | tf_op jit(solution)/shard_map/dot_general | solution.py:20
  270.7 5.0 %fusion.14 = bf16[1,2048,768]{2,1,0:T(8,128)(2,1)} fusion(f32[2048,768]{1,0:T(8,128)S(1)} %fusion.27, bf16[640,2048]{1,0:T(8,128)(2,1)S(1)} %copy-done.11, f32[640,768]{1,0:T(8,128)S(1)} %copy-done.36, f32[640,768]{1,0:T(8,128)S(1)} %copy-done.39, f32[640,768]{1,0:T(8,128)S(1)} %copy-done.37, f32[640]{0:T(1024)S(1)} %convert_reduce_fusion), kind=kOutput, calls=%fused_computation.18 | convolution fusion | flops 2021818368 | bytes 17959424 | tf_op jit(solution)/shard_map/dot_general | solution.py:20
  275.7 3.0 %fusion.25 = f32[2048,768]{1,0:T(8,128)S(1)} fusion(bf16[640,2176]{1,0:T(8,128)(2,1)S(1)} %copy-done.24, f32[640,768]{1,0:T(8,128)S(1)} %copy-done.42, f32[640,768]{1,0:T(8,128)S(1)} %copy-done.45, f32[640]{0:T(1024)S(1)} %convert_reduce_fusion.1), kind=kOutput, calls=%fused_computation.41 | convolution fusion | flops 2016706560 | bytes 12849152 | tf_op jit(solution)/shard_map/dot_general | solution.py:20
  278.7 4.7 %fusion.15 = bf16[1,2048,768]{2,1,0:T(8,128)(2,1)} fusion(f32[2048,768]{1,0:T(8,128)S(1)} %fusion.25, bf16[640,2048]{1,0:T(8,128)(2,1)S(1)} %copy-done.11, f32[640,768]{1,0:T(8,128)S(1)} %copy-done.36, f32[640,768]{1,0:T(8,128)S(1)} %copy-done.37, f32[640]{0:T(1024)S(1)} %convert_reduce_fusion), kind=kOutput, calls=%fused_computation.19 | convolution fusion | flops 2019852288 | bytes 15993344 | tf_op jit(solution)/shard_map/dot_general | solution.py:20
  (129 shorter events, 4.4 us)
Async XLA Ops:
  0.6 140.8 %copy-start = (bf16[1,768,2048]{2,1,0:T(8,128)(2,1)S(1)}, bf16[1,768,2048]{2,1,0:T(8,128)(2,1)}, u32[]{:S(2)}) copy-start(bf16[1,768,2048]{2,1,0:T(8,128)(2,1)} %param.21) | copy-start | bytes 9437188
  11.2 1.8 copy-start.16
  12.6 7.1 %copy-start.2 = (bf16[1,1,64,2048]{3,2,1,0:T(8,128)(2,1)S(1)}, bf16[1,1,64,2048]{3,2,1,0:T(8,128)(2,1)}, u32[]{:S(2)}) copy-start(bf16[1,1,64,2048]{3,2,1,0:T(8,128)(2,1)} %param.12) | copy-start | bytes 786436
  15.6 4.0 %copy-start.3 = (bf16[2,1,1,64,2048]{4,3,2,1,0:T(8,128)(2,1)S(1)}, bf16[2,1,1,64,2048]{4,3,2,1,0:T(8,128)(2,1)}, u32[]{:S(2)}) copy-start(bf16[2,1,1,64,2048]{4,3,2,1,0:T(8,128)(2,1)} %param.14) | copy-start | bytes 1572868
  15.7 4.0 %copy-start.4 = (bf16[1,1,1,64,2048]{4,3,2,1,0:T(8,128)(2,1)S(1)}, bf16[1,1,1,64,2048]{4,3,2,1,0:T(8,128)(2,1)}, u32[]{:S(2)}) copy-start(bf16[1,1,1,64,2048]{4,3,2,1,0:T(8,128)(2,1)} %param.13) | copy-start | bytes 786436
  16.5 113.1 %copy-start.25 = (pred[32]{0:T(512)(128)(4,1)S(1)}, pred[32]{0:T(512)(128)(4,1)}, u32[]{:S(2)}) copy-start(pred[32]{0:T(512)(128)(4,1)} %iota_compare_fusion.20) | copy-start | bytes 100
  16.5 113.1 %copy-start.33 = (bf16[2048,32]{0,1:T(8,128)(2,1)S(1)}, bf16[2048,32]{0,1:T(8,128)(2,1)}, u32[]{:S(2)}) copy-start(bf16[2048,32]{0,1:T(8,128)(2,1)} %param.15) | copy-start | bytes 393220
  129.6 11.8 %copy-start.5 = (bf16[640,2048]{1,0:T(8,128)(2,1)}, bf16[640,2048]{1,0:T(8,128)(2,1)S(1)}, u32[]{:S(2)}) copy-start(bf16[640,2048]{1,0:T(8,128)(2,1)S(1)} %get-tuple-element.23) | copy-start | bytes 7864324
  129.6 3.7 %copy-start.23 = (bf16[640,2176]{1,0:T(8,128)(2,1)S(1)}, bf16[640,2176]{1,0:T(8,128)(2,1)}, u32[]{:S(2)}) copy-start(bf16[640,2176]{1,0:T(8,128)(2,1)} %get-tuple-element.22) | copy-start | bytes 8355844
  129.6 4.3 %copy-start.17 = (s32[640]{0:T(1024)S(1)}, s32[640]{0:T(1024)}, u32[]{:S(2)}) copy-start(s32[640]{0:T(1024)} %copy-done.16) | copy-start | bytes 7684
  129.6 4.8 %copy-start.19 = (s32[640]{0:T(1024)S(1)}, s32[640]{0:T(1024)}, u32[]{:S(2)}) copy-start(s32[640]{0:T(1024)} %fusion.120) | copy-start | bytes 7684
  133.3 11.9 %copy-start.14 = (f32[640]{0:T(1024)}, f32[640]{0:T(1024)S(1)}, u32[]{:S(2)}) copy-start(f32[640]{0:T(1024)S(1)} %get-tuple-element.32) | copy-start | bytes 7684
  133.3 11.9 %copy-start.15 = (f32[640]{0:T(1024)}, f32[640]{0:T(1024)S(1)}, u32[]{:S(2)}) copy-start(f32[640]{0:T(1024)S(1)} %get-tuple-element.33) | copy-start | bytes 7684
  133.3 3.7 %copy-start.27 = (bf16[1,2048,768]{2,1,0:T(8,128)(2,1)S(1)}, bf16[1,2048,768]{2,1,0:T(8,128)(2,1)}, u32[]{:S(2)}) copy-start(bf16[1,2048,768]{2,1,0:T(8,128)(2,1)} %param.19) | copy-start | bytes 9437188
  133.4 11.8 %copy-start.6 = (f32[640,4]{1,0:T(8,128)}, f32[640,4]{1,0:T(8,128)S(1)}, u32[]{:S(2)}) copy-start(f32[640,4]{1,0:T(8,128)S(1)} %slice_convert_fusion.3) | copy-start | bytes 30724
  135.9 3.3 %copy-start.8 = (f32[640,4]{1,0:T(8,128)}, f32[640,4]{1,0:T(8,128)S(1)}, u32[]{:S(2)}) copy-start(f32[640,4]{1,0:T(8,128)S(1)} %slice_convert_fusion.2) | copy-start | bytes 30724
  137.0 2.2 copy-start.29
  139.2 2.2 copy-start.41
  141.4 3.8 %copy-start.43 = (f32[640,768]{1,0:T(8,128)}, f32[640,768]{1,0:T(8,128)S(1)}, u32[]{:S(2)}) copy-start(f32[640,768]{1,0:T(8,128)S(1)} %fusion.8) | copy-start | bytes 5898244
  145.2 1.2 copy-start.12
  223.9 3.0 %copy-start.26 = (pred[32]{0:T(512)(128)(4,1)S(1)}, pred[32]{0:T(512)(128)(4,1)}, u32[]{:S(2)}) copy-start(pred[32]{0:T(512)(128)(4,1)} %iota_compare_fusion.20) | copy-start | bytes 100
  223.9 3.0 %copy-start.34 = (bf16[2048,32]{0,1:T(8,128)(2,1)S(1)}, bf16[2048,32]{0,1:T(8,128)(2,1)}, u32[]{:S(2)}) copy-start(bf16[2048,32]{0,1:T(8,128)(2,1)} %param.15) | copy-start | bytes 393220
  226.9 5.1 %copy-start.10 = (bf16[640,2048]{1,0:T(8,128)(2,1)}, bf16[640,2048]{1,0:T(8,128)(2,1)S(1)}, u32[]{:S(2)}) copy-start(bf16[640,2048]{1,0:T(8,128)(2,1)S(1)} %add_convert_fusion.3) | copy-start | bytes 7864324
  226.9 2.9 %copy-start.28 = (bf16[1,2048,768]{2,1,0:T(8,128)(2,1)S(1)}, bf16[1,2048,768]{2,1,0:T(8,128)(2,1)}, u32[]{:S(2)}) copy-start(bf16[1,2048,768]{2,1,0:T(8,128)(2,1)} %param.19) | copy-start | bytes 9437188
  229.4 9.2 %copy-start.21 = (f32[640]{0:T(1024)}, f32[640]{0:T(1024)S(1)}, u32[]{:S(2)}) copy-start(f32[640]{0:T(1024)S(1)} %get-tuple-element.30) | copy-start | bytes 7684
  229.4 9.2 %copy-start.22 = (f32[640]{0:T(1024)}, f32[640]{0:T(1024)S(1)}, u32[]{:S(2)}) copy-start(f32[640]{0:T(1024)S(1)} %get-tuple-element.31) | copy-start | bytes 7684
  229.8 2.2 copy-start.30
  232.1 2.3 copy-start.35
  232.1 2.5 copy-start.31
  234.5 4.0 %copy-start.38 = (f32[640,768]{1,0:T(8,128)}, f32[640,768]{1,0:T(8,128)S(1)}, u32[]{:S(2)}) copy-start(f32[640,768]{1,0:T(8,128)S(1)} %fusion.6) | copy-start | bytes 5898244
  234.5 4.0 %copy-start.9 = (f32[640,4]{1,0:T(8,128)S(1)}, f32[640,4]{1,0:T(8,128)}, u32[]{:S(2)}) copy-start(f32[640,4]{1,0:T(8,128)} %copy-done.8) | copy-start | bytes 30724
  234.5 4.0 %copy-start.13 = (pred[640,1]{1,0:T(8,128)(4,1)S(1)}, pred[640,1]{1,0:T(8,128)(4,1)}, u32[]{:S(2)}) copy-start(pred[640,1]{1,0:T(8,128)(4,1)} %get-tuple-element.41) | copy-start | bytes 1924
  234.5 4.6 %copy-start.18 = (s32[640]{0:T(1024)S(1)}, s32[640]{0:T(1024)}, u32[]{:S(2)}) copy-start(s32[640]{0:T(1024)} %multiply_add_fusion) | copy-start | bytes 7684
  234.5 4.6 %copy-start.20 = (f32[640]{0:T(1024)S(1)}, f32[640]{0:T(1024)}, u32[]{:S(2)}) copy-start(f32[640]{0:T(1024)} %fusion.103) | copy-start | bytes 7684
  234.5 18.8 %copy-start.7 = (f32[640,4]{1,0:T(8,128)S(1)}, f32[640,4]{1,0:T(8,128)}, u32[]{:S(2)}) copy-start(f32[640,4]{1,0:T(8,128)} %copy-done.6) | copy-start | bytes 30724
  257.5 5.0 %copy-start.32 = (bf16[640,2048]{1,0:T(8,128)(2,1)S(1)}, bf16[640,2048]{1,0:T(8,128)(2,1)}, u32[]{:S(2)}) copy-start(bf16[640,2048]{1,0:T(8,128)(2,1)} %get-tuple-element.27) | copy-start | bytes 7864324
  257.5 5.0 %copy-start.40 = (bf16[640,768]{1,0:T(8,128)(2,1)S(1)}, bf16[640,768]{1,0:T(8,128)(2,1)}, u32[]{:S(2)}) copy-start(bf16[640,768]{1,0:T(8,128)(2,1)} %get-tuple-element.39) | copy-start | bytes 2949124
  262.5 4.6 %copy-start.24 = (bf16[640,2176]{1,0:T(8,128)(2,1)S(1)}, bf16[640,2176]{1,0:T(8,128)(2,1)}, u32[]{:S(2)}) copy-start(bf16[640,2176]{1,0:T(8,128)(2,1)} %get-tuple-element.22) | copy-start | bytes 8355844
  262.5 4.6 %copy-start.42 = (f32[640,768]{1,0:T(8,128)S(1)}, f32[640,768]{1,0:T(8,128)}, u32[]{:S(2)}) copy-start(f32[640,768]{1,0:T(8,128)} %copy-done.41) | copy-start | bytes 5898244
  262.5 4.6 %copy-start.44 = (f32[640,768]{1,0:T(8,128)S(1)}, f32[640,768]{1,0:T(8,128)}, u32[]{:S(2)}) copy-start(f32[640,768]{1,0:T(8,128)} %copy-done.43) | copy-start | bytes 5898244
  262.6 4.6 %copy-start.45 = (f32[640,768]{1,0:T(8,128)S(1)}, f32[640,768]{1,0:T(8,128)}, u32[]{:S(2)}) copy-start(f32[640,768]{1,0:T(8,128)} %get-tuple-element.56) | copy-start | bytes 5898244
  267.2 3.1 %copy-start.11 = (bf16[640,2048]{1,0:T(8,128)(2,1)S(1)}, bf16[640,2048]{1,0:T(8,128)(2,1)}, u32[]{:S(2)}) copy-start(bf16[640,2048]{1,0:T(8,128)(2,1)} %copy-done.10) | copy-start | bytes 7864324
  267.2 3.1 %copy-start.36 = (f32[640,768]{1,0:T(8,128)S(1)}, f32[640,768]{1,0:T(8,128)}, u32[]{:S(2)}) copy-start(f32[640,768]{1,0:T(8,128)} %copy-done.35) | copy-start | bytes 5898244
  267.2 3.1 %copy-start.37 = (f32[640,768]{1,0:T(8,128)S(1)}, f32[640,768]{1,0:T(8,128)}, u32[]{:S(2)}) copy-start(f32[640,768]{1,0:T(8,128)} %get-tuple-element.57) | copy-start | bytes 5898244
  267.2 3.5 %copy-start.39 = (f32[640,768]{1,0:T(8,128)S(1)}, f32[640,768]{1,0:T(8,128)}, u32[]{:S(2)}) copy-start(f32[640,768]{1,0:T(8,128)} %copy-done.38) | copy-start | bytes 5898244
  278.7 4.7 %copy-start.1 = (bf16[1,768,2048]{2,1,0:T(8,128)(2,1)S(1)}, bf16[1,768,2048]{2,1,0:T(8,128)(2,1)}, u32[]{:S(2)}) copy-start(bf16[1,768,2048]{2,1,0:T(8,128)(2,1)} %param.21) | copy-start | bytes 9437188
